TPU v7x, 32 devices: a whole 2x2x4 slice. The times are simulated.
32 devices in a mesh: head: 4 (over z), span: 8 (over y, x, core).
Axes of the slice: x: 2, y: 2, z: 4, core: 2. Of those that a mesh axis runs over, the one named last changes fastest.
Arguments:
- tokens: bfloat16 [8, 4096, 512], P('span', 'head'), may hold values from -6 to 6
- segment_ids: int32 [8, 4096], P('span'), may hold values from 0 to 4, as said below
- first_gain: float32 [512], P(('head', 'span')), may hold values from 0.5 to 1.5
- first_shift: float32 [512], P(('head', 'span')), may hold values from -3 to 3
- project_weight: bfloat16 [3, 512, 512], P(None, ('head', 'span')), may hold values from -0.25 to 0.25
- project_bias: float32 [3, 512], P(None, ('head', 'span')), may hold values from -1.2 to 1.2
- output_weight: bfloat16 [512, 512], P(('head', 'span')), may hold values from -1 to 1
- output_bias: float32 [512], P(('head', 'span')), may hold values from -3 to 3
- second_gain: float32 [512], P(('head', 'span')), may hold values from 0.5 to 1.5
- second_shift: float32 [512], P(('head', 'span')), may hold values from -3 to 3
- expand_weight: bfloat16 [512, 2048], P(('head', 'span')), may hold values from -0.25 to 0.25
- expand_bias: float32 [2048], P(('head', 'span')), may hold values from -3 to 3
- reduce_weight: bfloat16 [2048, 512], P(('head', 'span')), may hold values from -0.125 to 0.125
- reduce_bias: float32 [512], P(('head', 'span')), may hold values from -3 to 3
- cotangent: bfloat16 [8, 4096, 512], P('span', 'head'), may hold values from -6 to 6
Outputs:
- layer_output: bfloat16 [8, 4096, 512], P('span', 'head')
- tokens_grad: bfloat16 [8, 4096, 512], P('span', 'head')
- first_gain_grad: float32 [512], P(('head', 'span'))
- first_shift_grad: float32 [512], P(('head', 'span'))
- project_weight_grad: float32 [3, 512, 512], P(None, ('head', 'span'))
- project_bias_grad: float32 [3, 512], P(None, ('head', 'span'))
- output_weight_grad: float32 [512, 512], P(('head', 'span'))
- output_bias_grad: float32 [512], P(('head', 'span'))
- second_gain_grad: float32 [512], P(('head', 'span'))
- second_shift_grad: float32 [512], P(('head', 'span'))
- expand_weight_grad: float32 [512, 2048], P(('head', 'span'))
- expand_bias_grad: float32 [2048], P(('head', 'span'))
- reduce_weight_grad: float32 [2048, 512], P(('head', 'span'))
- reduce_bias_grad: float32 [512], P(('head', 'span'))
Inputs may be any that keep to these rules, and one draw needn't show every extreme that they name: `segment_ids`: row r is spans 2r and 2r+1 laid end to end (8192 positions). Along a row the ids rise from 1 without falling, and every row ends with one or more padding positions of id 0, the only zeros of the row.
All inputs are finite; a program needn't handle non-finite values.
Results may differ from a plain program's by a relative error of at most 0.039.
Values may be sent and summed in bfloat16 or wider, within the bound.
A program may use at most 320 MiB of HBM per device.

v0:
```python
import functools
import jax
import jax.numpy as jnp
from jax import lax
from jax.experimental import pallas as pl
from jax.experimental.pallas import tpu as pltpu
from jax.sharding import PartitionSpec as P

F32, BF16, I32 = jnp.float32, jnp.bfloat16, jnp.int32
MESH = pl.DeviceIdType.MESH
VMEM = pltpu.VMEM
NEG = -1e30
EPS = 1e-5
TOK = 1024
TILE = 256
D = 512
FF = 2048
EXT = 2384
SIZES = (1024, 512, 256, 128, 64, 32, 16)
EXT_AT = (0, 1056, 1600, 1888, 2048, 2144, 2208)
WIDE_AT = 2256
TRANS_B = (((1,), (1,)), ((), ()))
TRANS_A = (((0,), (0,)), ((), ()))


def mm(a, b):
    return jnp.dot(a, b, preferred_element_type=F32)


def mm_bt(a, b):
    return lax.dot_general(a, b, TRANS_B, preferred_element_type=F32)


def mm_at(a, b):
    return lax.dot_general(a, b, TRANS_A, preferred_element_type=F32)


def iota(shape, dim):
    return lax.broadcasted_iota(I32, shape, dim)


def split(v):
    high = v.astype(BF16)
    return high, (v - high.astype(F32)).astype(BF16)


def covers(t, c, block):
    if block == 0:
        return ((t & 255) >> 1) == c
    if block == 1:
        return ((t & 511) >> 2) == c
    if block == 2:
        return (t >> 3) == c
    level, start = mixed_levels(c)
    return (jnp.right_shift(t, level) == c - start) & (c < 124)


def mixed_levels(c):
    a, b, d, e = ((c >= edge).astype(I32) for edge in (64, 96, 112, 120))
    return 4 + a + b + d + e, 64 * a + 32 * b + 16 * d + 8 * e


def ones_where(cond):
    return jnp.where(cond, 1.0, 0.0).astype(BF16)


def identity(n):
    return ones_where(iota((n, n), 0) == iota((n, n), 1))


def fill_spread(spt):
    @pl.loop(0, TOK // TILE)
    def _(j):
        for block in range(4):
            t = iota((TILE, 128), 0) + j * TILE
            c = iota((TILE, 128), 1)
            spt[pl.ds(j * TILE, TILE), 128 * block:128 * block + 128] = ones_where(covers(t, c, block))


def fill_pool(sp):
    @pl.loop(0, TOK // TILE)
    def _(j):
        for block in range(4):
            t = iota((128, TILE), 1) + j * TILE
            c = iota((128, TILE), 0)
            sp[128 * block:128 * block + 128, pl.ds(pl.multiple_of(j * TILE, TILE), TILE)] = ones_where(covers(t, c, block))


TILES = TOK // TILE
BIAS_MIXED = 15 * 160
BIASES = BIAS_MIXED + 336


def tile_level(i):
    return 0 if i < 8 else 1 if i < 12 else 2 if i < 14 else 3


def tile_at(i):
    return 2048 if i == 15 else 128 * i + 32 * tile_level(i)


def tile_keys(i):
    return 336 if i == 15 else 160


def tile_times(i):
    if i < 15:
        return float(2 ** tile_level(i))
    level, _unused = mixed_levels(iota((1, 128), 1))
    return (1 << level).astype(F32)


INNER = (1, 2, 3, 4, 5, 6, 9, 10)
OUTER = (0, 7, 8, 11, 12, 13, 14, 15)


def labels_of(total, squares, times):
    return jnp.where(times * squares == total * total, total / times, 0.0)


def head_masks(rows):
    lane = iota((rows, 128), 1)
    return ones_where(lane < 64), ones_where(lane >= 64)


def by_head(x, masks):
    return jnp.concatenate([x * masks[0], x * masks[1]], axis=0)


def own_blocks(x):
    return jnp.concatenate([x[0:64, 0:128], x[64:128, 128:256]], axis=0)


def twice(x):
    return jnp.concatenate([x, x], axis=1)


def two_rows(a, b):
    row = iota((16, a.shape[1]), 0)
    return jnp.where(row == 0, a, jnp.where(row == 1, b, 0.0))


def lanes_of(g, base=0):
    return pl.ds(pl.multiple_of(base + g * 128, 128), 128)


def coarse_cols(ref, base, j):
    return jnp.concatenate([ref[:, base + 128 * j:base + 128 * j + 128],
                            ref[:, base + 512 + 128 * (j // 2):base + 640 + 128 * (j // 2)],
                            ref[:, base + 768:base + 1024]], axis=1)


def coarse_blocks():
    return ([(128 * j, 0, 256 * j, 256) for j in range(4)] + [(512 + 128 * j, 1, 512 * j, 512) for j in range(2)]
            + [(768, 2, 0, 1024), (896, 3, 0, 1024)])


def near_rows(side):
    o, i = iota((96, 128), 0), iota((96, 128), 1)
    level = (o >> 4) + 1
    block = i >> 4
    fine = jnp.maximum(block - 1, 0)
    value_out, value_in = (o >> 3) & 1, jnp.where(block < 2, block, (i >> 3) & 1)
    width, size = jnp.left_shift(1, fine), jnp.left_shift(1, level)
    if side == 0:
        start = ((o & 7) - 8) * size
        at = jnp.where(block < 2, (i & 15) - 16, (i & 7) - 16) * width
    else:
        start = (o & 7) * size
        at = jnp.where(block < 2, i & 15, (i & 7) + 8) * width
    inside = (value_out == value_in) & (at >= start) & (at + width <= start + size)
    share = jnp.where(value_out == 1, 1.0, width.astype(F32) / size.astype(F32))
    return jnp.where(inside, share, 0.0).astype(BF16)


def wide_rows(value):
    r, i = iota((128, 128), 0), iota((128, 128), 1)
    k, j = r & 15, (i & 15) - 8 * value
    own = ((r >> 4) == (i >> 4)) & (j >= 0) & (j < 8)
    fine, rough = own & (k < 8) & (j == k), own & (k >= 8) & (k < 12) & ((j >> 1) == k - 8)
    return jnp.where(fine, 1.0, jnp.where(rough, 1.0 if value else 0.5, 0.0)).astype(BF16)


def far_and_near(side, far, near):
    return jnp.concatenate([far, near] if side == 0 else [near, far], axis=0)


def border(side, l):
    return EXT_AT[l] + (16 + SIZES[l] if side else 0)


def own_border(side, l):
    return EXT_AT[l] + (SIZES[l] if side else 16)


def pick_far(side, rows):
    return rows[0:8] if side else rows[8:16]


def column_of(row, n):
    spread = jnp.where(iota((n, n), 0) == iota((n, n), 1), jnp.broadcast_to(row, (n, n)), 0.0)
    return jnp.broadcast_to(jnp.sum(spread, axis=1, keepdims=True), (n, 128)).astype(BF16)


def where_am_i():
    h = lax.axis_index("head")
    s = lax.axis_index("span")
    return h, s, s // 4, (s // 2) % 2, s % 2


class Peers:
    def __init__(self, near):
        h, s = lax.axis_index("head"), lax.axis_index("span")
        odd = s % 2
        self.place = odd * 4 + h
        self.odd = odd
        self.h = h
        other = s + 1 - 2 * odd
        self.z_index = [lax.rem(h + d, 4) for d in (1, 2, 3)]
        self.zs = [{"head": z} for z in self.z_index]
        self.core = {"span": other}
        opposite = {"head": 3 - h, "span": other}
        step = 1 - 2 * odd
        self.right = {"head": lax.rem(h + 1, 4), "span": s + step * ((h + 1) // 4)}
        self.left = {"head": lax.rem(h + 3, 4), "span": s + step * (1 - (h + 3) // 4)}
        self.greeted = self.zs + [self.core, opposite]
        if near:
            y, x = s // 4, (s // 2) % 2
            self.y, self.x, self.c = y, x, odd
            self.s = s
            self.px = {"span": y * 4 + (1 - x) * 2 + odd}
            self.py = {"span": (1 - y) * 4 + x * 2 + odd}
            self.s_index = [lax.rem(s + d, 8) for d in range(1, 8)]
            self.spans = [{"span": o} for o in self.s_index]
            self.greeted = self.zs + self.spans + [opposite]


def greet(devices):
    barrier = pltpu.get_barrier_semaphore()
    for d in devices:
        pl.semaphore_signal(barrier, inc=1, device_id=d, device_id_type=MESH)
    pl.semaphore_wait(barrier, len(devices))


def rcopy(src, dst, send, recv, device):
    return pltpu.make_async_remote_copy(src_ref=src, dst_ref=dst, send_sem=send, recv_sem=recv,
                                        device_id=device, device_id_type=MESH)


class Gather:
    def __init__(self, me, shard, full, swap, local, send, recv):
        self.me, self.shard, self.full, self.swap, self.local, self.send, self.recv = me, shard, full, swap, local, send, recv

    def own(self):
        m = self.me
        return pltpu.make_async_copy(self.shard, self.full(m.h, m.y, m.x, m.c), self.local)

    def hop(self, k):
        m, a = self.me, slice(None)
        if k < 3:
            return rcopy(self.shard, self.full(m.h, m.y, m.x, m.c), self.send.at[k], self.recv.at[k], m.zs[k])
        if k == 3:
            ref, dev = self.full(a, m.y, m.x, m.c), m.py if self.swap else m.px
        elif k == 4:
            ref, dev = (self.full(a, a, m.x, m.c), m.px) if self.swap else (self.full(a, m.y, a, m.c), m.py)
        else:
            ref, dev = self.full(a, a, a, m.c), m.core
        return rcopy(ref, ref, self.send.at[k], self.recv.at[k], dev)

    def start(self, stage):
        if stage == 0:
            self.own().start()
            for k in range(3):
                self.hop(k).start()
        else:
            self.hop(2 + stage).start()

    def wait(self, stage):
        if stage == 0:
            self.own().wait()
            for k in range(3):
                self.hop(k).wait()
        else:
            self.hop(2 + stage).wait()


class Scatter:
    def __init__(self, me, grad, mine, swap, bufs, send, recv):
        self.me, self.grad, self.mine, self.swap, self.bufs, self.send, self.recv = me, grad, mine, swap, bufs, send, recv

    def hops(self, stage):
        m, s, r = self.me, self.send, self.recv
        r1, r2, r3, r4 = self.bufs
        if stage == 0:
            return [rcopy(self.grad(1 - m.c), r1, s.at[0], r.at[0], m.core)]
        if stage == 1:
            src, dev = (r1.at[:, 1 - m.y], m.py) if self.swap else (r1.at[:, :, 1 - m.x], m.px)
            return [rcopy(src, r2, s.at[1], r.at[1], dev)]
        if stage == 2:
            src, dev = (r2.at[:, 1 - m.x], m.px) if self.swap else (r2.at[:, 1 - m.y], m.py)
            return [rcopy(src, r3, s.at[2], r.at[2], dev)]
        return [rcopy(r3.at[m.z_index[k]], r4.at[k], s.at[3 + k], r.at[3 + k], m.zs[k]) for k in range(3)]

    def start(self, stage):
        for cp in self.hops(stage):
            cp.start()

    def wait(self, stage):
        for cp in self.hops(stage):
            cp.wait()

    def add(self, stage):
        m = self.me
        r1, r2, r3, r4 = self.bufs

        def into(dst, key, other):
            dst[key] = (dst[key].astype(F32) + other.astype(F32)).astype(dst.dtype)
        if stage == 0:
            @pl.loop(0, 4)
            def _(hh):
                for yy in range(2):
                    for xx in range(2):
                        into(r1, (hh, yy, xx), self.mine(hh, yy, xx))
        elif stage == 1:
            @pl.loop(0, 4)
            def _(hh):
                for v in range(2):
                    into(r2, (hh, v), r1[hh, m.y, v] if self.swap else r1[hh, v, m.x])
        else:
            @pl.loop(0, 4)
            def _(hh):
                into(r3, (hh,), r2[hh, m.x if self.swap else m.y])

    def result(self):
        r1, r2, r3, r4 = self.bufs
        acc = r3[self.me.h].astype(F32)
        for k in range(3):
            acc = acc + r4[k].astype(F32)
        return acc


class SmallGather:
    def __init__(self, me, tile, full, local, send, recv):
        self.me, self.tile, self.full, self.local, self.send, self.recv = me, tile, full, local, send, recv

    def first(self):
        dst = self.full.at[self.me.h, self.me.s]
        return [rcopy(self.tile, dst, self.send.at[k], self.recv.at[k], self.me.zs[k]) for k in range(3)]

    def second(self):
        ref = self.full.at[:, self.me.s]
        return [rcopy(ref, ref, self.send.at[3 + k], self.recv.at[3 + k], self.me.spans[k]) for k in range(7)]

    def own(self):
        return pltpu.make_async_copy(self.tile, self.full.at[self.me.h, self.me.s], self.local)


class SmallScatter:
    def __init__(self, me, grad, got, total, got_z, send, recv):
        self.me, self.grad, self.got, self.total, self.got_z, self.send, self.recv = me, grad, got, total, got_z, send, recv

    def first(self):
        m = self.me
        return [rcopy(self.grad.at[:, m.s_index[k]], self.got.at[k], self.send.at[k], self.recv.at[k], m.spans[k]) for k in range(7)]

    def second(self):
        m = self.me
        return [rcopy(self.total.at[m.z_index[k]], self.got_z.at[k], self.send.at[7 + k], self.recv.at[7 + k], m.zs[k]) for k in range(3)]

    def add(self):
        v = self.grad[:, self.me.s]
        for k in range(7):
            v = v + self.got[k]
        self.total[...] = v

    def result(self):
        v = self.total[self.me.h]
        for k in range(3):
            v = v + self.got_z[k]
        return v


def start_all(copies):
    for cp in copies:
        cp.start()


def wait_all(copies):
    for cp in copies:
        cp.wait()


FFN_SHAPES = ((16, D), (16, 768), (16, 1280), (32, D), (32, D))


def ffn_index(k, whole):
    half = (k - 1) % 2
    if k == 0:
        return 0, ()
    if k < 3:
        return 1, (slice(None), whole(768 * half, 768 + 512 * half))
    return 2, (whole(32 * half, 32),)


def ffn_view(refs, k, index):
    which, tail = ffn_index(k, pl.ds)
    return refs[which].at[index + tail]


def ffn_values(refs, k, index):
    which, tail = ffn_index(k, lambda at, n: slice(at, at + n))
    return refs[which][index + tail]


def scatter_bufs(shape, dtype):
    return [VMEM((4, 2, 2) + shape, dtype), VMEM((4, 2) + shape, dtype), VMEM((4,) + shape, dtype), VMEM((3,) + shape, dtype)]


def split3(v):
    high, rest = split(v)
    mid = rest
    low = (v - high.astype(F32) - mid.astype(F32)).astype(BF16)
    return high, mid, low


def mm_exact(v, ones):
    a, b, c = split3(v)
    return mm(a, ones) + mm(b, ones) + mm(c, ones)


def small_rows(vt, g1, s1, pb, ob, g2, s2, rb, eb):
    vt[...] = jnp.zeros_like(vt)
    for r, ref in enumerate((g1, s1, None, None, None, ob, g2, s2)):
        vt[r:r + 1, 0:16] = pb[r - 2:r - 1, :] if ref is None else ref[...]
    vt[0:1, 16:32] = rb[...]
    for r in range(8):
        vt[r:r + 1, 32:40] = eb[0:1, 8 * r:8 * r + 8]


def unpack_small(gathered, vecs, b1):
    v = gathered[...].reshape(256, 128)
    row, n = iota((256, D), 0), iota((256, D), 1)
    lane, col = iota((128, D), 0), iota((128, D), 1)
    mine = (row >> 3) == (n >> 4)
    for half in range(2):
        x = mm_exact(v, ones_where(lane == (col & 15) + 16 * half))
        vecs[8 * half:8 * half + 8, :] = jnp.sum(jnp.where(mine, x, 0.0).reshape(32, 8, D), axis=0)
    x = mm_exact(v, ones_where(lane == (col & 7) + 32))
    for q in range(4):
        ok = ((row >> 3) == ((n + 512 * q) >> 6)) & ((row & 7) == ((n >> 3) & 7))
        b1[0:1, D * q:D * q + D] = jnp.sum(jnp.where(ok, x, 0.0), axis=0, keepdims=True)


def fill_bias(bias, labk, labq, place, tiles):
    def matching(i):
        kl = labk[tile_at(i):tile_at(i) + tile_keys(i), :].astype(F32)
        return (kl == labq[i:i + 1, :]) & (kl != 0.0)

    r, c = iota((160, 128), 0), iota((160, 128), 1)
    near = jnp.abs((r >> 4) - 1 - (c >> 4)) <= 1
    far = near & (jnp.abs((r >> 3) - 2 - (c >> 3)) >= 2)
    same = (r - 16) == c
    for i in tiles:
        if i == 15:
            continue
        ok = matching(i) & near | same if i < 8 else matching(i) & far
        bias[160 * i:160 * i + 160, :] = jnp.where(ok, 0.0, NEG)
    if 15 not in tiles:
        return
    r, c = iota((336, 128), 0), iota((336, 128), 1)
    inner = (r >= 96).astype(I32) + (r >= 160).astype(I32)
    start = jnp.where(inner == 0, 0, jnp.where(inner == 1, 96, 160))
    e, k = (r - 208) >> 4, (r - 208) & 15
    upper = (k >= 8).astype(I32)
    level_k = jnp.where(r < 208, 4 + inner, 7 + upper)
    pos_k = jnp.where(r < 208, r - start - 16, jnp.where(k < 8, e * 8 + k, e * 4 + k - 8))
    level_q, start_q = mixed_levels(c)
    pos_q = c - start_q + jnp.where(level_q == 7, place * 8, jnp.where(level_q == 8, place * 4, 0))
    shape = (level_k == level_q) & (jnp.abs((pos_k >> 4) - (pos_q >> 4)) <= 1) & (jnp.abs((pos_k >> 3) - (pos_q >> 3)) >= 2)
    bias[BIAS_MIXED:BIASES, :] = jnp.where(matching(15) & shape, 0.0, NEG)


def bias_of(bias, i):
    return twice(bias[160 * i:160 * i + 160, :] if i < 15 else bias[BIAS_MIXED:BIASES, :])


def forward_kernel(near, *refs):
    refs = list(refs)

    def take(n):
        out = refs[:n]
        del refs[:n]
        return out
    tok, seg = take(2)
    if near:
        wq_in, = take(1)
        small = take(8)
        ffn_in = take(3)
    else:
        wq, vecs = take(2)
    kvx_o, qx_o, bias_o, a1_o, ao_o, iz_o, sp_o, spt_o = take(8)
    if near:
        wq_o, vecs_o, b1_o = take(3)
        ffn_o = take(3)
    kvx, qx, bias, a1, ao, iz, sp, spt, xh, labq, n0, nc, z0, labk, seg2, msg, got, wbuf, out_sem, e_send, e_recv = take(21)
    if near:
        wq, vecs, b1, vt, vg, local, send, recv, send_v, recv_v = take(10)
    me = Peers(near)
    place = me.place
    outs = []

    def emit(src, dst):
        cp = pltpu.make_async_copy(src, dst, out_sem.at[len(outs)])
        cp.start()
        outs.append(cp)

    got[...] = jnp.zeros_like(got)
    if near:
        small_rows(vt, *small)
    greet(me.greeted)
    ids_core = rcopy(seg, seg2, e_send.at[6], e_recv.at[6], me.core)
    ids_core.start()
    if near:
        small_g = SmallGather(me, vt, vg, local.at[15], send_v, recv_v)
        small_g.own().start()
        start_all(small_g.first())
        first = []
        for k, (which, lanes) in enumerate((w, pl.ds(lo, 256)) for w in (pl.ds(1, 2), pl.ds(0, 1)) for lo in (0, 256)):
            first.append(Gather(me, wq_in.at[which, :, lanes], lambda h, y, x, c, which=which, lanes=lanes: wq.at[which, h, y, x, c, :, lanes],
                                k % 2 == 1, local.at[k], send.at[k], recv.at[k]))
        later = [Gather(me, ffn_view(ffn_in, k, ()), lambda h, y, x, c, k=k: ffn_view(ffn_o, k, (h, y, x, c)), k in (2, 4),
                        local.at[4 + k], send.at[4 + k], recv.at[4 + k]) for k in range(5)]

    def step(group, stage, *pieces):
        if not near:
            return
        for k in pieces:
            a = (first if group == 0 else later)[k]
            if stage >= 0:
                a.wait(stage)
            if stage < 3:
                a.start(stage + 1)

    step(0, -1, 0, 1, 2, 3)
    fill_pool(sp)
    fill_spread(spt)
    emit(sp, sp_o)
    emit(spt, spt_o)
    if near:
        small_g.own().wait()
        wait_all(small_g.first())
        start_all(small_g.second())
    step(0, 0, 0, 1, 2, 3)
    step(1, -1, 0, 1, 2, 3, 4)
    ids_core.wait()

    def chunk(ref, k):
        return ref[:, pl.ds(pl.multiple_of(TOK * k, TOK), TOK)].astype(F32)
    odd = me.odd.astype(F32)
    ids = chunk(seg, me.h)
    ids_left = jnp.where(me.h > 0, chunk(seg, lax.rem(me.h + 3, 4)), chunk(seg2, 3) * odd)
    ids_right = jnp.where(me.h < 3, chunk(seg, lax.rem(me.h + 1, 4)), chunk(seg2, 0) * (1.0 - odd))
    ids_b = jnp.broadcast_to(ids, (128, TOK)).astype(BF16)
    sq_b = jnp.broadcast_to(ids * ids, (128, TOK)).astype(BF16)
    eye = identity(TILE)
    for j in range(TILES):
        labk[16 + TILE * j:16 + TILE * j + TILE, :] = mm_bt(eye, ids_b[:, TILE * j:TILE * j + TILE]).astype(BF16)
    for i in range(8):
        labq[i:i + 1, :] = ids[:, 128 * i:128 * i + 128]
    row, t = iota((128, TOK), 0), iota((128, TOK), 1)
    level, level_row = row >> 4, iota((1, 128), 1) >> 4
    for side, v in ((0, ids_left), (1, ids_right)):
        base = jnp.right_shift(TOK, level) - 16 if side == 0 else 0
        sel = ones_where(jnp.right_shift(t, level) == base + (row & 15))
        x = mm_bt(two_rows(v, v * v).astype(BF16), sel)
        col = column_of(labels_of(x[0:1], x[1:2], jnp.left_shift(1, level_row).astype(F32)), 128)
        for l in range(7):
            labk[border(side, l):border(side, l) + 16, :] = col[16 * l:16 * l + 16]
    even_ids = [jnp.where(me.odd == 0, chunk(seg, k), chunk(seg2, k)) for k in range(4)]
    odd_ids = [jnp.where(me.odd == 0, chunk(seg2, k), chunk(seg, k)) for k in range(4)]
    all_ids = jnp.concatenate(even_ids + odd_ids, axis=0)
    x = mm_bt(jnp.concatenate([all_ids, all_ids * all_ids], axis=0).astype(BF16), sp[496:512, :])
    lab = labels_of(x[0:8], x[8:16], jnp.where(iota((8, 16), 1) < 8, 128.0, 256.0))
    lab = jnp.broadcast_to(lab[:, None, :], (8, 16, 16)).reshape(128, 16)
    lab = jnp.sum(jnp.where((iota((128, 16), 0) & 15) == iota((128, 16), 1), lab, 0.0), axis=1, keepdims=True)
    labk[WIDE_AT:EXT, :] = jnp.broadcast_to(lab, (128, 128)).astype(BF16)

    def put_coarse(dst, b, value, cols):
        at, block, _t, _n = coarse_blocks()[b]
        if block < 3:
            level = block + 1
            row = EXT_AT[level] + 16 + at - (0, 512, 768)[block]
            dst[row:row + 128, cols] = value
        else:
            for level, a, n in ((4, 0, 64), (5, 64, 32), (6, 96, 16)):
                dst[EXT_AT[level] + 16:EXT_AT[level] + 16 + n, cols] = value[a:a + n]

    for b, (at, block, t, n) in enumerate(coarse_blocks()):
        s = sp[128 * block:128 * block + 128, t:t + n]
        rows_level, _unused = mixed_levels(iota((128, 128), 0))
        cols_level, _unused = mixed_levels(iota((8, 128), 1))
        times_r = (1 << rows_level).astype(F32) if block == 3 else float(2 ** (block + 1))
        times_c = (1 << cols_level).astype(F32) if block == 3 else float(2 ** (block + 1))
        lab = labels_of(mm_bt(s, ids_b[:, t:t + n]), mm_bt(s, sq_b[:, t:t + n]), times_r)
        put_coarse(labk, b, lab.astype(BF16), slice(0, 128))
        row = labels_of(mm_bt(ids_b[0:8, t:t + n], s), mm_bt(sq_b[0:8, t:t + n], s), times_c)
        labq[8 + b:9 + b, :] = row[0:1, :]
    step(0, 1, 0, 1, 2, 3)
    fill_bias(bias, labk, labq, place, range(16))
    emit(bias, bias_o)
    @pl.loop(0, TILES)
    def _(j):
        rows = pl.ds(pl.multiple_of(TILE * j, TILE), TILE)
        v = tok[rows, :].astype(F32)
        center = v - jnp.mean(v, axis=-1, keepdims=True)
        xh[rows, :] = center * lax.rsqrt(jnp.mean(center * center, axis=-1, keepdims=True) + EPS)
    step(0, 2, 0, 1, 2, 3)
    step(1, 0, 0, 1, 2, 3, 4)
    if near:
        wait_all(small_g.second())
        unpack_small(vg, vecs, b1)
        emit(vecs, vecs_o)
        emit(b1, b1_o)
    @pl.loop(0, TILES)
    def _(j):
        rows = pl.ds(pl.multiple_of(TILE * j, TILE), TILE)
        a1[rows, :] = (xh[rows, :] * vecs[0:1, :] + vecs[1:2, :]).astype(BF16)
    emit(a1, a1_o)
    step(0, 3, 0, 1)

    def project(c):
        w = wq[c].reshape(D, D)
        for j in range(TILES):
            r = (mm(a1[TILE * j:TILE * j + TILE, :], w) + vecs[2 + c:3 + c, :]).astype(BF16)
            if c == 0:
                qx[TILE * j:TILE * j + TILE, :] = r * jnp.array(0.125, BF16)
            else:
                kvx[16 + TILE * j:16 + TILE * j + TILE, D * (c - 1):D * c] = r

    def pool_parts(block, t, n):
        if block == 3:
            level, _unused = mixed_levels(iota((128, D), 0))
            shrink = 1.0 / (1 << level).astype(F32)
        else:
            shrink = 0.5 ** (block + 1)
        return sp[128 * block:128 * block + 128, t:t + n], shrink
    project(1)
    project(2)
    step(1, 1, 0, 2)
    wide_z = [rcopy(wbuf.at[place], wbuf.at[place], e_send.at[2 + k], e_recv.at[2 + k], me.zs[k]) for k in range(3)]
    for b, (at, block, t, n) in reversed(list(enumerate(coarse_blocks()))):
        pool, shrink = pool_parts(block, t, n)
        kc, vc = mm(pool, kvx[16 + t:16 + t + n, 0:D]) * shrink, mm(pool, kvx[16 + t:16 + t + n, D:2 * D])
        put_coarse(kvx, b, kc.astype(BF16), slice(0, D))
        put_coarse(kvx, b, vc.astype(BF16), slice(D, 2 * D))
        if block == 3:
            wbuf[place] = jnp.concatenate([kc[112:120], vc[112:120]], axis=0).astype(BF16)
            start_all(wide_z)
    step(1, 1, 1)
    for side in range(2):
        for l in range(7):
            at = own_border(side, l)
            k16, v16 = kvx[at:at + 16, 0:D], kvx[at:at + 16, D:2 * D]
            if l == 0:
                msg[side, 0], msg[side, 1] = k16, v16
            else:
                far = [pick_far(side, v.astype(F32)) for v in (k16, v16)]
                msg[side, l + 1] = jnp.concatenate(far, axis=0).astype(BF16)
    to_right = rcopy(msg.at[1], got.at[0], e_send.at[0], e_recv.at[0], me.right)
    to_left = rcopy(msg.at[0], got.at[1], e_send.at[1], e_recv.at[1], me.left)
    four = wbuf.at[pl.ds(4 * me.odd, 4)]
    wide_core = rcopy(four, four, e_send.at[5], e_recv.at[5], me.core)
    not_last, not_first = place < 7, place > 0

    @pl.when(not_last)
    def _():
        to_right.start()

    @pl.when(not_first)
    def _():
        to_left.start()
    step(1, 1, 4)
    step(0, 3, 2, 3)
    project(0)
    for at, block, t, n in coarse_blocks():
        pool, shrink = pool_parts(block, t, n)
        qx[1024 + at:1024 + at + 128, :] = (mm(pool, qx[t:t + n, :]) * shrink).astype(BF16)
    emit(qx, qx_o)
    if near:
        emit(wq, wq_o)
    step(1, 1, 3)
    masks = head_masks(128)

    def tile(g, i):
        keys = slice(tile_at(i), tile_at(i) + tile_keys(i))
        kw, vw = kvx[keys, lanes_of(g)], kvx[keys, lanes_of(g, D)]
        q = by_head(qx[128 * i:128 * i + 128, lanes_of(g)], masks)
        e = jnp.exp(mm_bt(kw, q) + bias_of(bias, i))
        times = tile_times(i)
        z = jnp.sum(e, axis=0, keepdims=True)
        z0_, z1_ = z[:, 0:128] * times, z[:, 128:256] * times
        n = own_blocks(mm_at(vw, e.astype(BF16)))
        if i < 8:
            cols = slice(128 * i, 128 * i + 128)
            n0[g, :, cols] = n
            z0[g, 0:1, cols] = z0_
            z0[g, 1:2, cols] = z1_
        else:
            cols = slice(128 * i - 1024, 128 * i - 896)
            high, low = split(two_rows(z0_, z1_))
            nc[g, :, cols] = jnp.concatenate([n.astype(BF16), high, low], axis=0)

    @pl.loop(0, 4)
    def _(g):
        for k in range(4):
            @pl.when(g == k)
            def _():
                if k == 1:
                    wait_all(wide_z)
                    wide_core.start()
        for i in INNER:
            tile(g, i)

    wide_core.wait()
    w = wbuf[...].reshape(128, D)
    kvx[WIDE_AT:EXT, 0:D] = mm(wide_rows(0), w).astype(BF16)
    kvx[WIDE_AT:EXT, D:2 * D] = mm(wide_rows(1), w).astype(BF16)

    @pl.when(not_last)
    def _():
        to_right.wait_send()
        to_left.wait_recv()

    @pl.when(not_first)
    def _():
        to_left.wait_send()
        to_right.wait_recv()
    for side in range(2):
        m = got[side].reshape(128, D)
        closer = mm(near_rows(side), m)
        m = m.astype(F32)
        for l in range(7):
            at = border(side, l)
            if l == 0:
                k16, v16 = m[0:16], m[16:32]
            else:
                a, b = 16 * (l + 1), 16 * (l - 1)
                k16 = far_and_near(side, m[a:a + 8], closer[b:b + 8])
                v16 = far_and_near(side, m[a + 8:a + 16], closer[b + 8:b + 16])
            kvx[at:at + 16, 0:D] = k16.astype(BF16)
            kvx[at:at + 16, D:2 * D] = v16.astype(BF16)
    emit(kvx, kvx_o)

    @pl.loop(0, 4)
    def _(g):
        for k in range(4):
            @pl.when(g == k)
            def _():
                step(1, 2, *((0, 2), (1,), (), (4,))[k])
        for i in OUTER:
            tile(g, i)
        c_ref = nc.at[g]
        for j in range(TILES):
            cols = slice(TILE * j, TILE * j + TILE)
            r = mm(coarse_cols(c_ref, 0, j), sp[:, cols])
            n = n0[g, :, cols] + r[0:128]
            i0 = 1.0 / (z0[g, 0:1, cols] + r[128:129] + r[144:145])
            i1 = 1.0 / (z0[g, 1:2, cols] + r[129:130] + r[145:146])
            iz[g, 0:1, cols] = i0
            iz[g, 1:2, cols] = i1
            ao[pl.ds(pl.multiple_of(g * 128, 128), 64), cols] = (n[0:64] * i0).astype(BF16)
            ao[pl.ds(pl.multiple_of(g * 128 + 64, 64), 64), cols] = (n[64:128] * i1).astype(BF16)
    emit(ao, ao_o)
    emit(iz, iz_o)
    step(1, 2, 3)
    step(1, 3, 0, 1, 2, 3, 4)
    wait_all(outs)


ANY = pl.BlockSpec(memory_space=pl.ANY)
IN_VMEM = pl.BlockSpec(memory_space=pltpu.VMEM)
S = jax.ShapeDtypeStruct
SEM = pltpu.SemaphoreType.DMA


def forward(near, tok, seg, *params):
    grid = (4, 2, 2, 2)
    shapes = [S((EXT, 2 * D), BF16), S((2048, D), BF16), S((BIASES, 128), F32), S((TOK, D), BF16), S((D, TOK), BF16),
              S((4, 2, TOK), F32), S((512, TOK), BF16), S((TOK, 512), BF16)]
    scratch = [VMEM(s.shape, s.dtype) for s in shapes] + [
        VMEM((TOK, D), F32), VMEM((16, 128), F32), VMEM((4, 128, TOK), F32), VMEM((4, 160, TOK), BF16), VMEM((4, 2, TOK), F32),
        VMEM((EXT, 128), BF16), VMEM(seg.shape, I32), VMEM((2, 8, 16, D), BF16), VMEM((2, 8, 16, D), BF16), VMEM((8, 16, D), BF16),
        SEM((16,)), SEM((7,)), SEM((7,))]
    if near:
        shapes += [S((3,) + grid + (16, D), BF16), S((16, D), F32), S((1, FF), F32)]
        shapes += [S(grid + a.shape, a.dtype) for a in params[9:]]
        scratch += [VMEM((3,) + grid + (16, D), BF16), VMEM((16, D), F32), VMEM((1, FF), F32), VMEM((8, 128), F32),
                    VMEM((4, 8, 8, 128), F32), SEM((16,)), SEM((9, 6)), SEM((9, 6)), SEM((10,)), SEM((10,))]
        specs = [IN_VMEM] * 9 + [ANY] * 3
    else:
        specs = [IN_VMEM] * 2
    return pl.pallas_call(
        functools.partial(forward_kernel, near),
        out_shape=shapes,
        in_specs=[IN_VMEM, IN_VMEM] + specs,
        out_specs=[ANY] * len(shapes),
        scratch_shapes=scratch,
        compiler_params=pltpu.CompilerParams(collective_id=0, has_side_effects=True, vmem_limit_bytes=60 << 20),
        name="forward",
    )(tok, seg, *params)


C0 = 0.7978845608028654
C1 = 0.044715


def middle_kernel(tok, ao, cot, wo, w1, w2, vecs, b1, out, dh1_out, da_out, gwo, gw1, gw2, gvec, gb1,
                  awo, aw1, aw2, avec, ab1):
    j = pl.program_id(0)

    @pl.when(j == 0)
    def _():
        awo[...] = jnp.zeros_like(awo)
        aw1[...] = jnp.zeros_like(aw1)
        aw2[...] = jnp.zeros_like(aw2)
        avec[...] = jnp.zeros_like(avec)
        ab1[...] = jnp.zeros_like(ab1)
    mixed = ao[...]
    h1 = tok[...].astype(F32) + mm_at(mixed, wo[...]) + vecs[5:6, :]
    center = h1 - jnp.mean(h1, axis=-1, keepdims=True)
    inverse = lax.rsqrt(jnp.mean(center * center, axis=-1, keepdims=True) + EPS)
    xh = center * inverse
    gain = vecs[6:7, :]
    a2 = (xh * gain + vecs[7:8, :]).astype(BF16)
    dy = cot[...]
    y = h1 + vecs[8:9, :]
    da2 = jnp.zeros((512, D), F32)
    for k in range(FF // D):
        cols = slice(D * k, D * k + D)
        u = mm(a2, w1[:, cols]) + b1[:, cols]
        u2 = u * u
        th = jnp.tanh(u * (C0 + (C0 * C1) * u2))
        half = 0.5 * (1.0 + th)
        g = (u * half).astype(BF16)
        slope = half + 0.5 * u * (1.0 - th * th) * (C0 + (3.0 * C0 * C1) * u2)
        y = y + mm(g, w2[cols, :])
        du = (mm_bt(dy, w2[cols, :]) * slope).astype(BF16)
        aw2[cols, :] += mm_at(g, dy)
        aw1[:, cols] += mm_at(a2, du)
        ab1[:, cols] += jnp.sum(du.astype(F32), axis=0, keepdims=True)
        da2 = da2 + mm_bt(du, w1[:, cols])
    out[...] = y.astype(BF16)
    dyf = dy.astype(F32)
    e = da2 * gain
    dh1 = dyf + inverse * (e - jnp.mean(e, axis=-1, keepdims=True) - xh * jnp.mean(e * xh, axis=-1, keepdims=True))
    dh1_out[...] = dh1
    db = dh1.astype(BF16)
    awo[...] += mm(mixed, db)
    da_out[...] = mm_bt(wo[...], db).astype(BF16)
    avec[5:6, :] += jnp.sum(db.astype(F32), axis=0, keepdims=True)
    avec[6:7, :] += jnp.sum(da2 * xh, axis=0, keepdims=True)
    avec[7:8, :] += jnp.sum(da2, axis=0, keepdims=True)
    avec[8:9, :] += jnp.sum(dyf, axis=0, keepdims=True)

    @pl.when(j == TOK // 512 - 1)
    def _():
        gwo[...] = awo[...].astype(BF16)
        gw1[...] = aw1[...].astype(BF16)
        gw2[...] = aw2[...].astype(BF16)
        gvec[...] = avec[...]
        gb1[...] = ab1[...]


def whole(shape):
    return pl.BlockSpec(shape, lambda j: (0,) * len(shape), pipeline_mode=pl.Buffered(1))


def middle(tok, ao, cot, wo, w1, w2, vecs, b1):
    tile = pl.BlockSpec((512, D), lambda j: (j, 0))
    flat = pl.BlockSpec((D, 512), lambda j: (0, j))
    return pl.pallas_call(
        middle_kernel,
        grid=(TOK // 512,),
        out_shape=[S((TOK, D), BF16), S((TOK, D), F32), S((D, TOK), BF16), S((D, D), BF16), S((D, FF), BF16), S((FF, D), BF16),
                   S((16, D), F32), S((1, FF), F32)],
        in_specs=[tile, flat, tile, whole((D, D)), whole((D, FF)), whole((FF, D)), whole((16, D)), whole((1, FF))],
        out_specs=[tile, tile, flat, whole((D, D)), whole((D, FF)), whole((FF, D)), whole((16, D)), whole((1, FF))],
        scratch_shapes=[VMEM((D, D), F32), VMEM((D, FF), F32), VMEM((FF, D), F32), VMEM((16, D), F32), VMEM((1, FF), F32)],
        compiler_params=pltpu.CompilerParams(dimension_semantics=("arbitrary",), vmem_limit_bytes=60 << 20),
        name="middle",
    )(tok, ao, cot, wo, w1, w2, vecs, b1)


def pack_small(rows, b1):
    row, n = iota((256, D), 0), iota((256, D), 1)
    lane, col = iota((128, D), 0), iota((128, D), 1)
    mine = (row >> 3) == (n >> 4)

    def moved(v, ok, ones):
        total = None
        for part in split3(jnp.where(ok, v, 0.0)):
            r = mm_bt(part, ones)
            total = r if total is None else total + r
        return total
    eight = jnp.broadcast_to(rows[0:8][None], (32, 8, D)).reshape(256, D)
    out = moved(eight, mine, ones_where(lane == (col & 15)))
    out = out + moved(jnp.broadcast_to(rows[8:9], (256, D)), mine & ((row & 7) == 0), ones_where(lane == (col & 15) + 16))
    last = ones_where(lane == (col & 7) + 32)
    for q in range(4):
        ok = ((row >> 3) == ((n + 512 * q) >> 6)) & ((row & 7) == ((n >> 3) & 7))
        out = out + moved(jnp.broadcast_to(b1[0:1, D * q:D * q + D], (256, D)), ok, last)
    return out.reshape(4, 8, 8, 128)


def backward_kernel(near, *refs):
    refs = list(refs)

    def take(n):
        out = refs[:n]
        del refs[:n]
        return out
    ins = take(13)
    gffn, (gvec, gb1) = take(3), take(2)
    tok_o, gq_o = take(2)
    small_o = take(8 if near else 1)
    gffn_o = take(3 if near else 0)
    kvx, qx, bias, a1, ao, iz, sp, spt, da, tok, dh1, wq, vecs = take(13)
    gr, rm, dqt, dkv, dq, edge, e_got, w_all, w_got, w_mid, gq, avec, tok_s, dall, in_sem, out_sem, e_send, e_recv = take(18)
    if near:
        gv, f_mine, f_sem, send, recv, send_v, recv_v, v_got, v_sum, v_z = take(10)
        bufs = [take(4) for _ in range(11)]
    me = Peers(near)
    place = me.place
    loads = {}
    targets = (da, ao, iz, sp, kvx, qx, bias, spt, a1, tok, dh1, wq, vecs)
    names = ("da", "ao", "iz", "sp", "kvx", "qx", "bias", "spt", "a1", "tok", "dh1", "wq", "vecs")
    for k, name in enumerate(names):
        loads[name] = pltpu.make_async_copy(ins[k], targets[k], in_sem.at[k])
        loads[name].start()
    greet(me.greeted)
    mine_copies = []
    if near:
        for k in range(3):
            cp = pltpu.make_async_copy(gffn[k].at[:, :, :, me.c], f_mine[k], f_sem.at[k])
            cp.start()
            mine_copies.append(cp)
        every = slice(None)
        ffn = [Scatter(me, lambda c, k=k: ffn_view(gffn, k, (every, every, every, c)), lambda h, y, x, k=k: ffn_values(f_mine, k, (h, y, x)),
                       k in (2, 4), bufs[k], send.at[k], recv.at[k]) for k in range(5)]
        last = []
        for k in range(6):
            lo = 256 * (k % 2)
            last.append(Scatter(me, lambda c, k=k, lo=lo: gq.at[k // 2, :, :, :, c, :, pl.ds(lo, 256)],
                                lambda h, y, x, k=k, lo=lo: gq[k // 2, h, y, x, me.c, :, lo:lo + 256], k % 2 == 1,
                                bufs[5 + k], send.at[5 + k], recv.at[5 + k]))
        small_s = SmallScatter(me, gv, v_got, v_sum, v_z, send_v, recv_v)
        for a in ffn:
            a.start(0)

    def put_ffn(k):
        which, tail = ffn_index(k, lambda at, n: slice(at, at + n))
        gffn_o[which][tail or (slice(None),)] = ffn[k].result()

    def put_last(k):
        gq_o[k // 2, :, 256 * (k % 2):256 * (k % 2) + 256] = last[k].result()

    def step(group, stage, *pieces):
        if not near:
            return
        for k in pieces:
            a = (ffn if group == 0 else last)[k]
            a.wait(stage)
            if stage < 3:
                a.add(stage)
                a.start(stage + 1)
            elif group == 0:
                put_ffn(k)
            else:
                put_last(k)

    for name in ("da", "ao", "iz", "sp"):
        loads[name].wait()
    masks = head_masks(128)

    @pl.loop(0, 4)
    def _(g):
        lo, hi = pl.ds(pl.multiple_of(g * 128, 128), 64), pl.ds(pl.multiple_of(g * 128 + 64, 64), 64)
        for j in range(TILES):
            cols = slice(TILE * j, TILE * j + TILE)
            g0 = da[lo, cols].astype(F32) * iz[g, 0:1, cols]
            g1 = da[hi, cols].astype(F32) * iz[g, 1:2, cols]
            r0 = jnp.sum(g0 * ao[lo, cols].astype(F32), axis=0, keepdims=True)
            r1 = jnp.sum(g1 * ao[hi, cols].astype(F32), axis=0, keepdims=True)
            rm[g, 0:1, cols] = r0
            rm[g, 1:2, cols] = r1
            high, low = split(two_rows(r0, r1))
            gr[g, :, cols] = jnp.concatenate([g0.astype(BF16), g1.astype(BF16), high, low], axis=0)
        for b, (at, block, t, n) in enumerate(coarse_blocks()):
            x = mm_bt(gr[g, :, t:t + n], sp[128 * block:128 * block + 128, t:t + n])
            cols = slice(1024 + at, 1152 + at)
            gr[g, 0:128, cols] = x[0:128].astype(BF16)
            times = tile_times(8 + b)
            rm[g, 0:1, cols] = (x[128:129] + x[144:145]) * times
            rm[g, 1:2, cols] = (x[129:130] + x[145:146]) * times
    dkv[...] = jnp.zeros_like(dkv)
    for name in ("kvx", "qx", "bias"):
        loads[name].wait()
    zero = jnp.zeros((64, 128), BF16)

    def tile(g, i):
        keys = slice(tile_at(i), tile_at(i) + tile_keys(i))
        cols = slice(128 * i, 128 * i + 128)
        kw, vw = kvx[keys, lanes_of(g)], kvx[keys, lanes_of(g, D)]
        q = by_head(qx[cols, lanes_of(g)], masks)
        gt = gr[g, 0:128, cols]
        gb = jnp.concatenate([jnp.concatenate([gt[0:64], zero], axis=1), jnp.concatenate([zero, gt[64:128]], axis=1)], axis=0)
        e = jnp.exp(mm_bt(kw, q) + bias_of(bias, i))
        rest = jnp.concatenate([rm[g, 0:1, cols], rm[g, 1:2, cols]], axis=1)
        ds = (e * (mm(vw, gb) - rest)).astype(BF16)
        dkv[keys, lanes_of(g)] += mm(ds, q)
        dkv[keys, lanes_of(g, D)] += mm_bt(e.astype(BF16), gb)
        dqt[g, :, cols] = (own_blocks(mm_at(kw, ds)) * (0.125 / tile_times(i))).astype(BF16)

    if near:
        wait_all(mine_copies)
    step(0, 0, 0, 1, 2, 3, 4)

    @pl.loop(0, 4)
    def _(g):
        for i in OUTER:
            tile(g, i)
    for side in range(2):
        base, closer = [], []
        for l in range(7):
            at = border(side, l)
            k16, v16 = dkv[at:at + 16, 0:D], dkv[at:at + 16, D:2 * D]
            if l == 0:
                base += [k16, v16]
            elif side == 0:
                base += [k16[0:8], v16[0:8]]
                closer += [k16[8:16], v16[8:16]]
            else:
                base += [k16[8:16], v16[8:16]]
                closer += [k16[0:8], v16[0:8]]
        folded = mm_at(near_rows(side), jnp.concatenate(closer, axis=0).astype(BF16))
        edge[side] = (jnp.concatenate(base, axis=0) + folded).astype(BF16).reshape(8, 16, D)
    d_wide = mm_at(wide_rows(0), dkv[WIDE_AT:EXT, 0:D].astype(BF16)) + mm_at(wide_rows(1), dkv[WIDE_AT:EXT, D:2 * D].astype(BF16))
    w_all[...] = d_wide.astype(BF16).reshape(8, 16, D)
    to_right = rcopy(edge.at[1], e_got.at[0], e_send.at[0], e_recv.at[0], me.right)
    to_left = rcopy(edge.at[0], e_got.at[1], e_send.at[1], e_recv.at[1], me.left)
    wide_core = rcopy(w_all.at[pl.ds(4 * (1 - me.odd), 4)], w_mid, e_send.at[2], e_recv.at[2], me.core)
    not_last, not_first = place < 7, place > 0
    wide_core.start()

    @pl.when(not_last)
    def _():
        to_right.start()

    @pl.when(not_first)
    def _():
        to_left.start()
    step(0, 1, 0, 1, 2)

    @pl.loop(0, 2)
    def _(g):
        for i in INNER:
            tile(g, i)
    wide_core.wait()
    for k in range(4):
        w_mid[k] = (w_mid[k].astype(F32) + w_all[4 * me.odd + k].astype(F32)).astype(BF16)
    wide_z = [rcopy(w_mid.at[me.z_index[k]], w_got.at[k], e_send.at[3 + k], e_recv.at[3 + k], me.zs[k]) for k in range(3)]
    start_all(wide_z)

    @pl.loop(2, 4)
    def _(g):
        for i in INNER:
            tile(g, i)
    step(0, 1, 3, 4)

    @pl.loop(0, 4)
    def _(g):
        d_ref = dqt.at[g]
        eye = identity(TILE)
        for j in range(TILES):
            cols = slice(TILE * j, TILE * j + TILE)
            r = d_ref[:, cols].astype(F32) + mm(coarse_cols(d_ref, 1024, j), sp[:, cols])
            dq[cols, lanes_of(g)] = mm_bt(eye, r.astype(BF16)).astype(BF16)
    for name in ("spt", "a1", "tok", "dh1", "wq", "vecs"):
        loads[name].wait()
    avec[...] = jnp.zeros_like(avec)

    def projection_grad(c, d):
        aw = mm_at(a1[...], d).astype(BF16)
        avec[2 + c:3 + c, :] = jnp.sum(d.astype(F32), axis=0, keepdims=True)
        gq[c] = aw.reshape(4, 2, 2, 2, 16, D)
        if near:
            for a in last[2 * c:2 * c + 2]:
                a.start(0)
    projection_grad(0, dq[...])
    step(0, 2, 0, 1, 2)
    for cp in wide_z:
        cp.wait()

    def add_edge(side):
        m = e_got[side].reshape(128, D).astype(F32)
        for l in range(7):
            if l == 0:
                at, n = own_border(side, 0), 16
            else:
                at, n = own_border(side, l) + (0 if side else 8), 8
            a = 16 * (l + 1) if l else 0
            dkv[at:at + n, 0:D] += m[a:a + n]
            dkv[at:at + n, D:2 * D] += m[a + n:a + 2 * n]

    @pl.when(not_last)
    def _():
        to_right.wait_send()
        to_left.wait_recv()
        add_edge(1)

    @pl.when(not_first)
    def _():
        to_left.wait_send()
        to_right.wait_recv()
        add_edge(0)
    v = w_mid[me.h].astype(F32)
    for k in range(3):
        v = v + w_got[k].astype(F32)
    v = jnp.concatenate([v[0:8] * 0.5 ** 7, v[8:16]], axis=1)
    w_own = jnp.concatenate([v, jnp.zeros((8, 2 * D), F32)], axis=0).astype(BF16)
    lane_all = iota((1, 2 * D), 1)

    def coarse_rows(at, n, level):
        return (dkv[at:at + n, :] * jnp.where(lane_all < D, 0.5 ** level, 1.0)).astype(BF16)
    top = jnp.concatenate([coarse_rows(EXT_AT[3] + 16, 128, 3), coarse_rows(EXT_AT[4] + 16, 64, 4), coarse_rows(EXT_AT[5] + 16, 32, 5),
                           coarse_rows(EXT_AT[6] + 16, 16, 6), w_own], axis=0)
    for j in range(TILES):
        rows = slice(TILE * j, TILE * j + TILE)
        x = jnp.concatenate([coarse_rows(EXT_AT[1] + 16 + 128 * j, 128, 1), coarse_rows(EXT_AT[2] + 16 + 128 * (j // 2), 128, 2), top], axis=0)
        dall[rows, :] = (dkv[16 + TILE * j:16 + TILE * j + TILE, :] + mm(spt[rows, :], x)).astype(BF16)
    projection_grad(1, dall[:, 0:D])
    step(0, 2, 3, 4)
    step(1, 0, 0, 1)
    projection_grad(2, dall[:, D:2 * D])
    step(1, 0, 2, 3)
    @pl.loop(0, TILES)
    def _(j):
        rows = pl.ds(pl.multiple_of(TILE * j, TILE), TILE)
        da1 = mm_bt(dq[rows, :], wq[0].reshape(D, D)) + mm_bt(dall[rows, 0:D], wq[1].reshape(D, D)) + mm_bt(dall[rows, D:2 * D], wq[2].reshape(D, D))
        v = tok[rows, :].astype(F32)
        center = v - jnp.mean(v, axis=-1, keepdims=True)
        inverse = lax.rsqrt(jnp.mean(center * center, axis=-1, keepdims=True) + EPS)
        n = center * inverse
        e = da1 * vecs[0:1, :]
        dv = inverse * (e - jnp.mean(e, axis=-1, keepdims=True) - n * jnp.mean(e * n, axis=-1, keepdims=True))
        tok_s[rows, :] = (dh1[rows, :] + dv).astype(BF16)
        avec[0:1, :] += jnp.sum(da1 * n, axis=0, keepdims=True)
        avec[1:2, :] += jnp.sum(da1, axis=0, keepdims=True)
        for k, what in enumerate(((0, 4, 5), (1, 0, 1), (1, 2, 3))):
            @pl.when(j == k)
            def _():
                step(1, *what)
    done = pltpu.make_async_copy(tok_s, tok_o, out_sem.at[0])
    done.start()
    if not near:
        gq_o[...] = gq[...]
        small_o[0][...] = avec[...]
        done.wait()
        return
    avec[5:9, :] = gvec[5:9, :]
    gv[...] = pack_small(avec[...], gb1)
    start_all(small_s.first())
    step(1, 1, 4, 5)
    step(1, 2, 0, 1)
    wait_all(small_s.first())
    small_s.add()
    start_all(small_s.second())
    step(1, 2, 2, 3, 4, 5)
    step(0, 3, 0, 1, 2, 3, 4)
    step(1, 3, 0, 1, 2, 3, 4, 5)
    wait_all(small_s.second())
    t = small_s.result()
    for k, r in enumerate((0, 1, None, 5, 6, 7)):
        if r is None:
            small_o[k][...] = t[2:5, 0:16]
        else:
            small_o[k][...] = t[r:r + 1, 0:16]
    for r in range(8):
        small_o[6][0:1, 8 * r:8 * r + 8] = t[r:r + 1, 32:40]
    small_o[7][...] = t[0:1, 16:32]
    done.wait()


def backward(near, saved, wq, vecs, tok, da, dh1, gffn, gvec, gb1):
    kvx, qx, bias, a1, ao, iz, sp, spt = saved
    grid = (4, 2, 2, 2)
    vm = [VMEM(v.shape, v.dtype) for v in (kvx, qx, bias, a1, ao, iz, sp, spt, da, tok, dh1, wq, vecs)]
    scratch = vm + [VMEM((4, 160, 2048), BF16), VMEM((4, 2, 2048), F32), VMEM((4, 128, 2048), BF16), VMEM((EXT, 2 * D), F32),
                    VMEM((TOK, D), BF16), VMEM((2, 8, 16, D), BF16), VMEM((2, 8, 16, D), BF16), VMEM((8, 16, D), BF16),
                    VMEM((3, 16, D), BF16), VMEM((4, 16, D), BF16), VMEM((3,) + grid + (16, D), BF16), VMEM((16, D), F32), VMEM((TOK, D), BF16), VMEM((TOK, 2 * D), BF16),
                    SEM((13,)), SEM((1,)), SEM((6,)), SEM((6,))]
    if near:
        gffn = [g.reshape(grid + (g.shape[0] // 32, g.shape[1])) for g in gffn]
        shapes = [S((TOK, D), BF16), S((3, 16, D), F32)]
        shapes += [S((1, 16), F32), S((1, 16), F32), S((3, 16), F32), S((1, 16), F32), S((1, 16), F32), S((1, 16), F32), S((1, 64), F32), S((1, 16), F32)]
        shapes += [S(g.shape[4:], F32) for g in gffn]
        pieces = [(shape, BF16) for shape in FFN_SHAPES] + [((16, 256), BF16)] * 6
        scratch += [VMEM((4, 8, 8, 128), F32), [VMEM((4, 2, 2) + g.shape[4:], BF16) for g in gffn], SEM((3,)), SEM((11, 6)), SEM((11, 6)),
                    SEM((10,)), SEM((10,)), VMEM((7, 4, 8, 128), F32), VMEM((4, 8, 128), F32), VMEM((3, 8, 128), F32)]
        for shape, kind in pieces:
            scratch += scatter_bufs(shape, kind)
    else:
        gffn = gffn[0:3]
        shapes = [S((TOK, D), BF16), S((3,) + grid + (16, D), BF16), S((16, D), F32)]
    ordered = (da, ao, iz, sp, kvx, qx, bias, spt, a1, tok, dh1, wq, vecs)
    return pl.pallas_call(
        functools.partial(backward_kernel, near),
        out_shape=shapes,
        in_specs=[ANY] * 16 + [IN_VMEM] * 2,
        out_specs=[ANY] + [IN_VMEM] * (len(shapes) - 1),
        scratch_shapes=scratch,
        compiler_params=pltpu.CompilerParams(collective_id=1, has_side_effects=True, vmem_limit_bytes=62 << 20),
        name="backward",
    )(*ordered, *gffn, gvec, gb1)


def finish_kernel(n, *refs):
    for k in range(n):
        refs[n + k][...] = refs[k][...]


def finish(*values):
    n = len(values)
    return pl.pallas_call(
        functools.partial(finish_kernel, n),
        out_shape=[S(v.shape, v.dtype) for v in values],
        in_specs=[IN_VMEM] * n,
        out_specs=[IN_VMEM] * n,
        name="finish",
    )(*values)


BOTH = ("head", "span")


def shards(tokens, segment_ids, first_gain, first_shift, project_weight, project_bias, output_weight, output_bias,
           second_gain, second_shift, expand_weight, expand_bias, reduce_weight, reduce_bias, cotangent):
    tok, cot = tokens[0], cotangent[0]
    near = lax.axis_size("head") == 4 and lax.axis_size("span") == 8
    if near:
        vectors = (first_gain, first_shift, project_bias, output_bias, second_gain, second_shift, reduce_bias, expand_bias)
        vectors = [v if v.ndim == 2 else v[None] for v in vectors]
        *saved, wq, vecs, b1, wo, w1, w2 = forward(True, tok, segment_ids, project_weight, *vectors, output_weight, expand_weight, reduce_weight)
        wo, w1, w2 = wo.reshape(D, D), w1.reshape(D, FF), w2.reshape(FF, D)
    else:
        def full(v, axis=0):
            return lax.all_gather(v, BOTH, axis=axis, tiled=True)
        wq, wo, w1, w2 = full(project_weight, 1), full(output_weight), full(expand_weight), full(reduce_weight)
        rows = [full(first_gain), full(first_shift), *full(project_bias, 1), full(output_bias), full(second_gain), full(second_shift), full(reduce_bias)]
        vecs = jnp.pad(jnp.stack(rows), ((0, 7), (0, 0)))
        b1 = full(expand_bias)[None]
        saved = forward(False, tok, segment_ids, wq, vecs)
    ao = saved[4]
    out, dh1, da, *gffn, gvec, gb1 = middle(tok, ao, cot, wo, w1, w2, vecs, b1)
    dtok, gwq, *rest = backward(near, saved, wq, vecs, tok, da, dh1, gffn, gvec, gb1)
    if near:
        dtok, gwq, *rest = finish(dtok, gwq, *rest)
        small, (gwo, gw1, gw2) = rest[0:8], rest[8:11]
        small = [v if v.shape[0] == 3 else v.reshape(-1) for v in small]
    else:
        def part(v, axis=0):
            return lax.psum_scatter(v.astype(F32), BOTH, scatter_dimension=axis, tiled=True)
        vec, gwq = rest[0], gwq.reshape(3, D, D)
        gwq, gwo, gw1, gw2 = part(gwq, 1), part(gffn[0]), part(gffn[1]), part(gffn[2])
        small = (part(vec[0]), part(vec[1]), part(vec[2:5], 1), part(gvec[5]), part(gvec[6]), part(gvec[7]), part(gb1[0]), part(gvec[8]))
    return (out[None], dtok[None], small[0], small[1], gwq, small[2], gwo, small[3], small[4], small[5], gw1, small[6], gw2, small[7])


def solution(mesh):
    token, row, matrix = P("span", "head", None), P(BOTH), P(BOTH, None)
    three, bias = P(None, BOTH, None), P(None, BOTH)
    params = (row, row, three, bias, matrix, row, row, row, matrix, row, matrix, row)
    return jax.shard_map(shards, mesh=mesh, in_specs=(token, P("span", None)) + params + (token,),
                         out_specs=(token, token) + params, check_vma=False)
```

profile of v0, /device:TPU:0, one launch (start us, length us, event | category | flops | bytes accessed | tf_op | source)
XLA Modules:
  0.0 131.9 jit_solution(18349514957768898296)
XLA Ops:
  0.7 51.8 %forward.1 = (bf16[2384,1024]{1,0:T(8,128)(2,1)}, bf16[2048,512]{1,0:T(8,128)(2,1)}, f32[2736,128]{1,0:T(8,128)}, bf16[1024,512]{1,0:T(8,128)(2,1)}, bf16[512,10...) custom-call(bf16[1024,512]{1,0:T(8,128)(2,1)} %bitcast.24, ...), custom_call_target="tpu_custom_call" | custom-call | tf_op jit(solution)/shard_map/forward/pallas_call | solution.py:802
  52.5 25.9 %middle.1 = (bf16[1024,512]{1,0:T(8,128)(2,1)}, f32[1024,512]{1,0:T(8,128)}, bf16[512,1024]{1,0:T(8,128)(2,1)}, bf16[512,512]{1,0:T(8,128)(2,1)}, bf16[512,2048]...) custom-call(bf16[1024,512]{1,0:T(8,128)(2,1)} %bitcast.25, ...), custom_call_target="tpu_custom_call" | custom-call | tf_op jit(solution)/shard_map/middle/pallas_call | solution.py:881
  78.4 50.8 %backward.1 = (bf16[1024,512]{1,0:T(8,128)(2,1)}, f32[3,16,512]{2,1,0:T(8,128)}, f32[1,16]{1,0:T(1,128)}, f32[1,16]{1,0:T(1,128)}, f32[3,16]{1,0:T(4,128)}, /*in...) custom-call(bf16[512,1024]{1,0:T(8,128)(2,1)} %get-tuple-element.69., ...), custom_call_target="tpu_custom_call" | custom-call | tf_op jit(solution)/shard_map/backward/pallas_call | solution.py:1216
  129.2 2.5 %finish.1 = (bf16[1024,512]{1,0:T(8,128)(2,1)}, f32[3,16,512]{2,1,0:T(8,128)}, f32[1,16]{1,0:T(1,128)}, f32[1,16]{1,0:T(1,128)}, f32[3,16]{1,0:T(4,128)}, /*inde...) custom-call(bf16[1024,512]{1,0:T(8,128)(2,1)} %get-tuple-element.84., ...), custom_call_target="tpu_custom_call" | custom-call | tf_op jit(solution)/shard_map/finish/pallas_call | solution.py:1234
where the time goes:
time: 132 us
  Pallas kernels  131 us (99%)
    pallas_call x1, Pallas kernels, forward(): pl.pallas_call(functools.partial(forward_kernel, near), out_shape=shapes,...  51.8 us
    pallas_call x1, Pallas kernels, backward(): pl.pallas_call(functools.partial(backward_kernel, near), out_shape=shapes...  50.8 us
    pallas_call x1, Pallas kernels, middle(): pl.pallas_call(middle_kernel, grid=(TOK // 512,), out_shape=[S((TOK, D),...  25.9 us

commit v1 on v0

--- a/solution.py
+++ b/solution.py
@@ -608,6 +608,7 @@
     step(0, 1, 0, 1, 2, 3)
     fill_bias(bias, labk, labq, place, range(16))
     emit(bias, bias_o)
+    step(1, 0, 0, 1, 2)
     @pl.loop(0, TILES)
     def _(j):
         rows = pl.ds(pl.multiple_of(TILE * j, TILE), TILE)
@@ -615,7 +616,7 @@
         center = v - jnp.mean(v, axis=-1, keepdims=True)
         xh[rows, :] = center * lax.rsqrt(jnp.mean(center * center, axis=-1, keepdims=True) + EPS)
     step(0, 2, 0, 1, 2, 3)
-    step(1, 0, 0, 1, 2, 3, 4)
+    step(1, 0, 3, 4)
     if near:
         wait_all(small_g.second())
         unpack_small(vg, vecs, b1)

time: 132 us -> 131 us (level)
  no operation moved by 1% of the time
where the time goes in v1:
time: 131 us
  Pallas kernels  130 us (99%)
    pallas_call x1, Pallas kernels, forward(): pl.pallas_call(functools.partial(forward_kernel, near), out_shape=shapes,...  51.4 us
    pallas_call x1, Pallas kernels, backward(): pl.pallas_call(functools.partial(backward_kernel, near), out_shape=shapes...  50.4 us
    pallas_call x1, Pallas kernels, middle(): pl.pallas_call(middle_kernel, grid=(TOK // 512,), out_shape=[S((TOK, D),...  25.9 us

profile of v1, /device:TPU:0, one launch (start us, length us, event | category | flops | bytes accessed | tf_op | source)
XLA Modules:
  0.0 131.1 jit_solution(6026047379439545746)
XLA Ops:
  0.7 51.4 %forward.1 = (bf16[2384,1024]{1,0:T(8,128)(2,1)}, bf16[2048,512]{1,0:T(8,128)(2,1)}, f32[2736,128]{1,0:T(8,128)}, bf16[1024,512]{1,0:T(8,128)(2,1)}, bf16[512,10...) custom-call(bf16[1024,512]{1,0:T(8,128)(2,1)} %bitcast.24, ...), custom_call_target="tpu_custom_call" | custom-call | tf_op jit(solution)/shard_map/forward/pallas_call | solution.py:803
  52.1 25.9 %middle.1 = (bf16[1024,512]{1,0:T(8,128)(2,1)}, f32[1024,512]{1,0:T(8,128)}, bf16[512,1024]{1,0:T(8,128)(2,1)}, bf16[512,512]{1,0:T(8,128)(2,1)}, bf16[512,2048]...) custom-call(bf16[1024,512]{1,0:T(8,128)(2,1)} %bitcast.25, ...), custom_call_target="tpu_custom_call" | custom-call | tf_op jit(solution)/shard_map/middle/pallas_call | solution.py:882
  78.0 50.4 %backward.1 = (bf16[1024,512]{1,0:T(8,128)(2,1)}, f32[3,16,512]{2,1,0:T(8,128)}, f32[1,16]{1,0:T(1,128)}, f32[1,16]{1,0:T(1,128)}, f32[3,16]{1,0:T(4,128)}, /*in...) custom-call(bf16[512,1024]{1,0:T(8,128)(2,1)} %get-tuple-element.69., ...), custom_call_target="tpu_custom_call" | custom-call | tf_op jit(solution)/shard_map/backward/pallas_call | solution.py:1217
  128.5 2.5 %finish.1 = (bf16[1024,512]{1,0:T(8,128)(2,1)}, f32[3,16,512]{2,1,0:T(8,128)}, f32[1,16]{1,0:T(1,128)}, f32[1,16]{1,0:T(1,128)}, f32[3,16]{1,0:T(4,128)}, /*inde...) custom-call(bf16[1024,512]{1,0:T(8,128)(2,1)} %get-tuple-element.84., ...), custom_call_target="tpu_custom_call" | custom-call | tf_op jit(solution)/shard_map/finish/pallas_call | solution.py:1235
